TPU v7x, 512 devices: a whole 4x8x8 slice. The times are simulated.
512 devices in a mesh: grp: 8 (over x, core), blk: 64 (over y, z).
Axes of the slice: x: 4, y: 8, z: 8, core: 2. Of those that a mesh axis runs over, the one named last changes fastest.
Arguments:
- features: bfloat16 [65536, 256], P(('grp', 'blk')), may hold values from -6 to 6
- dest: int32 [65536, 1], P(('grp', 'blk')), may hold values from 0 to 63; in each aligned block of 128 rows (0 to 127, 128 to 255, ...) at most 4 rows name the same one
- placement: int32 [512, 256], P(('grp', 'blk')), may hold values from 0 to 255, each once within a row
- weight: bfloat16 [27, 256, 128], replicated, may hold values from -0.078125 to 0.078125
- grad_out: bfloat16 [64, 512, 4, 128], P('grp', 'blk'), may hold values from -6 to 6
Outputs:
- output: bfloat16 [64, 512, 4, 128], P('grp', 'blk')
- grad_rows: bfloat16 [65536, 256], P(('grp', 'blk'))
- weight_grad: bfloat16 [27, 256, 128], replicated
Inputs may be any that keep to these rules, and one draw needn't show every extreme that they name: `dest`: among the rows of one device no value is named by more than 4 rows, a bound that some block reaches. `placement`: each row is a permutation of 0 to 255.
All inputs are finite; a program needn't handle non-finite values.
Results may differ from a plain program's by a relative error of at most 0.0013.
Values may be sent and summed in bfloat16 or wider, within the bound.
A program may use at most 64 MiB of HBM per device.

v0:
```python
import math
import jax
import jax.numpy as jnp
from jax import lax
from jax.sharding import PartitionSpec as P


def extended(cells, sides, width):
    for axis, dim in sides:
        count = lax.axis_size(axis)
        ends = count - 1
        head = lax.slice_in_dim(cells, 0, width, axis=dim)
        tail = lax.slice_in_dim(cells, cells.shape[dim] - width, cells.shape[dim], axis=dim)
        cells = jnp.concatenate(
            [
                lax.ppermute(tail, axis, [(i, (i + 1) % count) for i in range(ends)]),
                cells,
                lax.ppermute(head, axis, [((i + 1) % count, i) for i in range(ends)]),
            ],
            axis=dim,
        )
    return cells


def shards(features, dest, placement, weight, grad_out):
    row_count, channels = features.shape
    blk_count = lax.axis_size("blk")
    grp_count = lax.axis_size("grp")
    voxel_of_slot = placement[0]
    voxel_count = voxel_of_slot.shape[0]
    capacity = voxel_count // blk_count
    size_x, size_y, size_z, out_channels = grad_out.shape
    target = dest[:, 0]
    owners = jnp.arange(blk_count, dtype=jnp.int32)
    one_hot = (target[:, None] == owners[None, :]).astype(jnp.int32)
    slot_rank = jnp.sum((jnp.cumsum(one_hot, axis=0) - one_hot) * one_hot, axis=1)
    send_counts = jnp.sum(one_hot, axis=0).reshape(blk_count, 1)
    slot_index = target * capacity + slot_rank
    outgoing = jnp.zeros((voxel_count, channels), jnp.bfloat16).at[slot_index].set(features)
    incoming, recv_counts = (
        lax.all_to_all(
            outgoing.reshape(blk_count, capacity, channels),
            "blk",
            split_axis=0,
            concat_axis=0,
            tiled=True,
        ),
        lax.all_to_all(send_counts, "blk", split_axis=0, concat_axis=0, tiled=True),
    )
    filled = (
        (jnp.arange(capacity, dtype=jnp.int32)[None, :] < recv_counts)
        .reshape(-1)
        .astype(jnp.float32)
    )
    voxel_rows = (
        jnp.zeros((voxel_count, channels), jnp.bfloat16)
        .at[voxel_of_slot]
        .set(incoming.reshape(voxel_count, channels))
    )
    occupied = jnp.zeros((voxel_count,), jnp.float32).at[voxel_of_slot].set(filled)[:, None]
    voxel_grid = voxel_rows.reshape(size_x, size_y, size_z, channels)
    padded = extended(voxel_grid, (("grp", 0), ("blk", 1)), 1)
    padded = jnp.pad(padded, ((0, 0), (0, 0), (1, 1), (0, 0)))
    shifted = []
    total = jnp.zeros((voxel_count, out_channels), jnp.float32)
    for offset in range(27):
        shift_x, shift_y, shift_z = (offset // 9, offset // 3 % 3, offset % 3)
        window = padded[
            shift_x : shift_x + size_x, shift_y : shift_y + size_y, shift_z : shift_z + size_z
        ].reshape(voxel_count, channels)
        shifted.append(window)
        total = total + jnp.dot(window, weight[offset], preferred_element_type=jnp.float32)
    output = (total * occupied).astype(jnp.bfloat16).reshape(size_x, size_y, size_z, out_channels)
    masked_grad = (
        grad_out.reshape(voxel_count, out_channels).astype(jnp.float32) * occupied
    ).astype(jnp.bfloat16)
    grad_padded = extended(
        masked_grad.reshape(size_x, size_y, size_z, out_channels), (("grp", 0), ("blk", 1)), 1
    )
    grad_padded = jnp.pad(grad_padded, ((0, 0), (0, 0), (1, 1), (0, 0)))
    back_total = jnp.zeros((voxel_count, channels), jnp.float32)
    partials = []
    for offset in range(27):
        shift_x, shift_y, shift_z = (offset // 9, offset // 3 % 3, offset % 3)
        window = grad_padded[
            2 - shift_x : 2 - shift_x + size_x,
            2 - shift_y : 2 - shift_y + size_y,
            2 - shift_z : 2 - shift_z + size_z,
        ].reshape(voxel_count, out_channels)
        back_total = back_total + lax.dot_general(
            window, weight[offset], (((1,), (1,)), ((), ())), preferred_element_type=jnp.float32
        )
        partials.append(
            lax.dot_general(
                shifted[offset],
                masked_grad,
                (((0,), (0,)), ((), ())),
                preferred_element_type=jnp.float32,
            )
        )
    grad_grid = (back_total * occupied).astype(jnp.bfloat16)
    weight_terms = jnp.stack(partials).reshape(27 * channels, out_channels)
    grad_scale = 1.0 / math.sqrt(row_count * blk_count * grp_count)
    weight_grad = (lax.psum(weight_terms, ("grp", "blk")) * grad_scale).astype(jnp.bfloat16)
    weight_grad = weight_grad.reshape(27, channels, out_channels)
    returning = grad_grid[voxel_of_slot].reshape(blk_count, capacity, channels)
    returned = lax.all_to_all(returning, "blk", split_axis=0, concat_axis=0, tiled=True)
    grad_rows = returned.reshape(voxel_count, channels)[slot_index]
    return (output, grad_rows, weight_grad)


def solution(mesh):
    in_specs = (
        P(("grp", "blk"), None),
        P(("grp", "blk"), None),
        P(("grp", "blk"), None),
        P(),
        P("grp", "blk", None, None),
    )
    out_specs = (P("grp", "blk", None, None), P(("grp", "blk"), None), P())
    return jax.shard_map(shards, mesh=mesh, in_specs=in_specs, out_specs=out_specs, check_vma=False)
```

profile of v0, /device:TPU:24, one launch (start us, length us, event | category | flops | bytes accessed | tf_op | source)
XLA Modules:
  0.0 480.3 jit_solution(8768574311076272875)
XLA Ops:
  9.6 16.4 %all-to-all-start.1 = ((s32[64,1,1]{2,1,0:T(1,128)}), s32[64,1,1]{2,1,0:T(1,128)S(1)}, u32[]{:S(2)}, u32[]{:S(2)}) async-start(s32[64,1,1]{2,1,0:T(1,128)} %copy.183), calls=%async_computation.1 | async-start | bytes 65536 | tf_op jit(solution)/shard_map/all_to_all | solution.py:48
  29.5 5.8 %all-to-all-done.1 = s32[64,1,1]{2,1,0:T(1,128)S(1)} async-done(((s32[64,1,1]{2,1,0:T(1,128)}), s32[64,1,1]{2,1,0:T(1,128)S(1)}, u32[]{:S(2)}, u32[]{:S(2)}) %all-to-all-start.1) | async-done | bytes 288 | tf_op jit(solution)/shard_map/all_to_all | solution.py:48
  35.3 7.3 %all-to-all-start = ((bf16[64,4,256]{2,1,0:T(4,128)(2,1)}), bf16[64,4,256]{2,1,0:T(4,128)(2,1)S(1)}, u32[]{:S(2)}, u32[]{:S(2)}) async-start(bf16[64,4,256]{2,1,0:T(4,128)(2,1)} %reshape.379), calls=%async_computation | async-start | bytes 262144 | tf_op jit(solution)/shard_map/all_to_all | solution.py:41
  47.8 3.0 collective-permute-start.4
  51.8 3.4 collective-permute-start.6
  55.2 4.6 collective-permute-start.7
  68.6 1.9 collective-permute-start
  72.5 12.3 %all-to-all-start.2 = ((bf16[64,4,256]{2,1,0:T(4,128)(2,1)}), bf16[64,4,256]{2,1,0:T(4,128)(2,1)S(1)}, u32[]{:S(2)}, u32[]{:S(2)}) async-start(bf16[64,4,256]{2,1,0:T(4,128)(2,1)} %reshape.436), calls=%async_computation.2 | async-start | bytes 262144 | tf_op jit(solution)/shard_map/all_to_all | solution.py:107
  86.4 4.1 collective-permute-done.1
  90.6 3.4 collective-permute-start.2
  93.9 4.8 collective-permute-start.3
  119.0 1.6 copy.176
  122.2 1.6 copy.175
  128.6 1.6 copy.172
  131.8 1.6 copy.170
  133.4 1.6 reshape.396
  138.2 1.6 copy.168
  141.4 1.6 copy.167
  144.6 1.6 copy.165
  154.9 1.6 reshape.387
  161.3 1.6 reshape.384
  182.7 1.8 copy-done.2
  188.6 281.5 %all-reduce.4.cloned.1.call-done = f32[6912,128]{1,0:T(8,128)} async-done(((f32[6912,128]{1,0:T(8,128)}), f32[6912,128]{1,0:T(8,128)}) %all-reduce.4.cloned.1.call-update) | async-done | bytes 3538960 | tf_op jit(solution)/shard_map/psum | solution.py:104
  470.1 3.4 multiply_convert_fusion
  (246 shorter events, 95.4 us)
Async XLA Ops:
  9.6 25.6 %all-to-all-start.1 = ((s32[64,1,1]{2,1,0:T(1,128)}), s32[64,1,1]{2,1,0:T(1,128)S(1)}, u32[]{:S(2)}, u32[]{:S(2)}) async-start(s32[64,1,1]{2,1,0:T(1,128)} %copy.183), calls=%async_computation.1 | async-start | bytes 65536 | tf_op jit(solution)/shard_map/all_to_all | solution.py:48
  35.3 31.7 %all-to-all-start = ((bf16[64,4,256]{2,1,0:T(4,128)(2,1)}), bf16[64,4,256]{2,1,0:T(4,128)(2,1)S(1)}, u32[]{:S(2)}, u32[]{:S(2)}) async-start(bf16[64,4,256]{2,1,0:T(4,128)(2,1)} %reshape.379), calls=%async_computation | async-start | bytes 262144 | tf_op jit(solution)/shard_map/all_to_all | solution.py:41
  42.6 19.2 %copy-start = (bf16[27,256,128]{2,1,0:T(8,128)(2,1)S(1)}, bf16[27,256,128]{2,1,0:T(8,128)(2,1)}, u32[]{:S(2)}) copy-start(bf16[27,256,128]{2,1,0:T(8,128)(2,1)} %param.8) | copy-start | bytes 5308420
  46.5 5.3 %collective-permute-start.5 = (bf16[1,8,4,128]{3,2,1,0:T(4,128)(2,1)S(1)}, bf16[1,8,4,128]{3,2,1,0:T(4,128)(2,1)S(1)}, u32[]{:S(2)}, u32[]{:S(2)}) collective-permute-start(bf16[1,8,4,128]{3,2,1,0:T(4,128)(2,1)S(1)} %bitcast.495), channel_id=1, source_target_pairs={{64,0},{128,64},{192,128},{256,192},{320,256},{384,320},{448,384},... | collective-permute-start | bytes 24584 | tf_op jit(solution)/shard_map/ppermute | solution.py:18
  47.8 4.0 collective-permute-start.4
  51.8 8.0 %collective-permute-start.6 = (bf16[10,1,4,128]{3,2,1,0:T(4,128)(2,1)S(1)}, bf16[10,1,4,128]{3,2,1,0:T(4,128)(2,1)S(1)}, u32[]{:S(2)}, u32[]{:S(2)}) collective-permute-start(bf16[10,1,4,128]{3,2,1,0:T(4,128)(2,1)S(1)} %get-tuple-element.65), channel_id=1, source_target_pairs={{0,1},{1,2},{2,3},{3,4},{4,5},{5,6},{6,7},{7,8},{8,9},{9,10},{10,1... | collective-permute-start | bytes 30728 | tf_op jit(solution)/shard_map/ppermute | solution.py:16
  55.2 5.9 %collective-permute-start.7 = (bf16[10,1,4,128]{3,2,1,0:T(4,128)(2,1)S(1)}, bf16[10,1,4,128]{3,2,1,0:T(4,128)(2,1)S(1)}, u32[]{:S(2)}, u32[]{:S(2)}) collective-permute-start(bf16[10,1,4,128]{3,2,1,0:T(4,128)(2,1)S(1)} %get-tuple-element.66), channel_id=1, source_target_pairs={{1,0},{2,1},{3,2},{4,3},{5,4},{6,5},{7,6},{8,7},{9,8},{10,9},{11,1... | collective-permute-start | bytes 30728 | tf_op jit(solution)/shard_map/ppermute | solution.py:18
  68.6 17.7 %collective-permute-start = (bf16[1,8,4,256]{3,1,2,0:T(8,128)(2,1)S(1)}, bf16[1,8,4,256]{3,1,2,0:T(8,128)(2,1)S(1)}, u32[]{:S(2)}, u32[]{:S(2)}) collective-permute-start(bf16[1,8,4,256]{3,1,2,0:T(8,128)(2,1)S(1)} %copy.152), channel_id=1, source_target_pairs={{0,64},{64,128},{128,192},{192,256},{256,320},{320,384},{384,448},... | collective-permute-start | bytes 49160 | tf_op jit(solution)/shard_map/ppermute | solution.py:16
  72.5 27.1 %all-to-all-start.2 = ((bf16[64,4,256]{2,1,0:T(4,128)(2,1)}), bf16[64,4,256]{2,1,0:T(4,128)(2,1)S(1)}, u32[]{:S(2)}, u32[]{:S(2)}) async-start(bf16[64,4,256]{2,1,0:T(4,128)(2,1)} %reshape.436), calls=%async_computation.2 | async-start | bytes 262144 | tf_op jit(solution)/shard_map/all_to_all | solution.py:107
  84.9 385.2 %all-reduce.4.cloned.1.call-start = ((), (), s32[]{:S(2)}) async-start(), calls=%async_computation.3 | async-start | bytes 7077888 | tf_op jit(solution)/shard_map/psum | solution.py:104
  85.0 13.8 %copy-start.18 = (bf16[8,8,4,256]{3,2,1,0:T(4,128)(2,1)}, bf16[8,8,4,256]{3,2,1,0:T(4,128)(2,1)S(1)}, u32[]{:S(2)}) copy-start(bf16[8,8,4,256]{3,2,1,0:T(4,128)(2,1)S(1)} %reshape.381) | copy-start | bytes 393220
  85.0 5.5 %collective-permute-start.1 = (bf16[1,8,4,256]{3,1,2,0:T(8,128)(2,1)S(1)}, bf16[1,8,4,256]{3,1,2,0:T(8,128)(2,1)S(1)}, u32[]{:S(2)}, u32[]{:S(2)}) collective-permute-start(bf16[1,8,4,256]{3,1,2,0:T(8,128)(2,1)S(1)} %copy.153), channel_id=1, source_target_pairs={{64,0},{128,64},{192,128},{256,192},{320,256},{384,320},{448,384},... | collective-permute-start | bytes 49160 | tf_op jit(solution)/shard_map/ppermute | solution.py:18
  86.4 14.8 %copy-start.31 = (bf16[9,8,4,256]{3,1,2,0:T(8,128)(2,1)}, bf16[9,8,4,256]{3,1,2,0:T(8,128)(2,1)S(1)}, u32[]{:S(2)}) copy-start(bf16[9,8,4,256]{3,1,2,0:T(8,128)(2,1)S(1)} %get-tuple-element.53) | copy-start | bytes 442372
  90.5 8.3 %copy-start.27 = (bf16[9,8,4,256]{3,1,2,0:T(8,128)(2,1)}, bf16[9,8,4,256]{3,1,2,0:T(8,128)(2,1)S(1)}, u32[]{:S(2)}) copy-start(bf16[9,8,4,256]{3,1,2,0:T(8,128)(2,1)S(1)} %get-tuple-element.71) | copy-start | bytes 442372
  90.6 10.6 %collective-permute-start.2 = (bf16[10,1,4,256]{3,1,2,0:T(2,128)(2,1)S(1)}, bf16[10,1,4,256]{3,1,2,0:T(2,128)(2,1)S(1)}, u32[]{:S(2)}, u32[]{:S(2)}) collective-permute-start(bf16[10,1,4,256]{3,1,2,0:T(2,128)(2,1)S(1)} %get-tuple-element.50), channel_id=1, source_target_pairs={{0,1},{1,2},{2,3},{3,4},{4,5},{5,6},{6,7},{7,8},{8,9},{9,10},{10,1... | collective-permute-start | bytes 61448 | tf_op jit(solution)/shard_map/ppermute | solution.py:16
  93.9 7.2 %collective-permute-start.3 = (bf16[10,1,4,256]{3,1,2,0:T(2,128)(2,1)S(1)}, bf16[10,1,4,256]{3,1,2,0:T(2,128)(2,1)S(1)}, u32[]{:S(2)}, u32[]{:S(2)}) collective-permute-start(bf16[10,1,4,256]{3,1,2,0:T(2,128)(2,1)S(1)} %get-tuple-element.51), channel_id=1, source_target_pairs={{1,0},{2,1},{3,2},{4,3},{5,4},{6,5},{7,6},{8,7},{9,8},{10,9},{11,1... | collective-permute-start | bytes 61448 | tf_op jit(solution)/shard_map/ppermute | solution.py:18
  154.9 15.8 %copy-start.8 = (bf16[256,256]{1,0:T(8,128)(2,1)S(1)}, bf16[256,256]{1,0:T(8,128)(2,1)}, u32[]{:S(2)}) copy-start(bf16[256,256]{1,0:T(8,128)(2,1)} %reshape.386) | copy-start | bytes 393220
  166.2 4.7 copy-start.17
  166.2 4.9 %copy-start.16 = (bf16[256,256]{1,0:T(8,128)(2,1)S(1)}, bf16[256,256]{1,0:T(8,128)(2,1)}, u32[]{:S(2)}) copy-start(bf16[256,256]{1,0:T(8,128)(2,1)} %reshape.388) | copy-start | bytes 393220
  166.2 5.1 %copy-start.11 = (bf16[256,256]{1,0:T(8,128)(2,1)S(1)}, bf16[256,256]{1,0:T(8,128)(2,1)}, u32[]{:S(2)}) copy-start(bf16[256,256]{1,0:T(8,128)(2,1)} %reshape.389) | copy-start | bytes 393220
  166.2 5.3 %copy-start.15 = (bf16[256,256]{1,0:T(8,128)(2,1)S(1)}, bf16[256,256]{1,0:T(8,128)(2,1)}, u32[]{:S(2)}) copy-start(bf16[256,256]{1,0:T(8,128)(2,1)} %reshape.390) | copy-start | bytes 393220
  167.3 4.3 copy-start.14
  168.4 3.4 copy-start.10
  169.5 2.5 copy-start.13
  (21 other events, 24.7 us)
Sparse Core Ops, SparseCore 0:
  184.6 285.4 all-reduce.3
where the time goes:
time: 482 us; the launch traced here: 480 us
  waiting for transfers between devices  293 us (61%)
  local copies, waits for them, and re-layouts  80.7 us (17%)
  starting transfers between devices  59.6 us (12%)
  matrix products  20.7 us (4%)
  between operations  15.2 us (3%)
  other arithmetic  11.4 us (2%)
    psum x1, waiting for transfers between devices, shards(): lax.psum(weight_terms, ('grp', 'blk')) * grad_scale  282 us
    slice x29, local copies, waits for them, and re-layouts, shards(): padded[shift_x:shift_x + size_x, shift_y:shift_y + size_y, shift_z:shift_...  32.4 us
    reshape x26, local copies, waits for them, and re-layouts, shards(): window = padded[shift_x:shift_x + size_x, shift_y:shift_y + size_y, shift...  30.6 us
    all_to_all x1, starting transfers between devices, shards(): lax.all_to_all(send_counts, 'blk', split_axis=0, concat_axis=0, tiled=True)  16.4 us
    all_to_all x1, starting transfers between devices, shards(): lax.all_to_all(returning, 'blk', split_axis=0, concat_axis=0, tiled=True)  12.3 us
    ppermute x4, starting transfers between devices, extended(): lax.ppermute(head, axis, [((i + 1) % count, i) for i in range(ends)])  11.9 us
    ppermute x4, starting transfers between devices, extended(): lax.ppermute(tail, axis, [(i, (i + 1) % count) for i in range(ends)])  11.7 us
  transfers between devices with their start and end apart: 12, of which 4 were waited for; matrix products, arithmetic and copies ran while one was open for 4% of the time, Pallas kernels for 0%

commit v1 on v0

--- a/solution.py
+++ b/solution.py
@@ -101,7 +101,7 @@
     grad_grid = (back_total * occupied).astype(jnp.bfloat16)
     weight_terms = jnp.stack(partials).reshape(27 * channels, out_channels)
     grad_scale = 1.0 / math.sqrt(row_count * blk_count * grp_count)
-    weight_grad = (lax.psum(weight_terms, ("grp", "blk")) * grad_scale).astype(jnp.bfloat16)
+    weight_grad = (lax.psum(lax.psum(weight_terms, "grp"), "blk") * grad_scale).astype(jnp.bfloat16)
     weight_grad = weight_grad.reshape(27, channels, out_channels)
     returning = grad_grid[voxel_of_slot].reshape(blk_count, capacity, channels)
     returned = lax.all_to_all(returning, "blk", split_axis=0, concat_axis=0, tiled=True)

time: 482 us -> 431 us (0.89)
  the two profiles are of different devices: /device:TPU:24 before, /device:TPU:2 now
where the time goes in v1:
time: 431 us; the launch traced here: 429 us
  waiting for transfers between devices  239 us (55%)
  local copies, waits for them, and re-layouts  68.4 us (16%)
  starting transfers between devices  53.2 us (12%)
  matrix products  42.2 us (10%)
  between operations  15.1 us (4%)
  other arithmetic  11.4 us (3%)
    psum x1, waiting for transfers between devices, shards(): lax.psum(lax.psum(weight_terms, 'grp'), 'blk') * grad_scale  146 us
    psum x1, waiting for transfers between devices, shards(): lax.psum(weight_terms, 'grp')  74.8 us
    reshape x26, local copies, waits for them, and re-layouts, shards(): window = padded[shift_x:shift_x + size_x, shift_y:shift_y + size_y, shift...  29 us
    slice x29, local copies, waits for them, and re-layouts, shards(): padded[shift_x:shift_x + size_x, shift_y:shift_y + size_y, shift_z:shift_...  27.4 us
    dot_general x27, matrix products, shards(): lax.dot_general(shifted[offset], masked_grad, (((0,), (0,)), ((), ())), p...  24.7 us
    all_to_all x1, starting transfers between devices, shards(): lax.all_to_all(send_counts, 'blk', split_axis=0, concat_axis=0, tiled=True)  16.6 us
    all_to_all x1, starting transfers between devices, shards(): lax.all_to_all(returning, 'blk', split_axis=0, concat_axis=0, tiled=True)  13 us
    dot_general x27, matrix products, shards(): jnp.dot(window, weight[offset], preferred_element_type=jnp.float32)  12.5 us
  transfers between devices with their start and end apart: 13, of which 7 were waited for; matrix products, arithmetic and copies ran while one was open for 12% of the time, Pallas kernels for 0%

profile of v1, /device:TPU:2, one launch (start us, length us, event | category | flops | bytes accessed | tf_op | source)
XLA Modules:
  0.0 429.4 jit_solution(12504599183733194274)
XLA Ops:
  9.6 16.6 %all-to-all-start.1 = ((s32[64,1,1]{2,1,0:T(1,128)}), s32[64,1,1]{2,1,0:T(1,128)S(1)}, u32[]{:S(2)}, u32[]{:S(2)}) async-start(s32[64,1,1]{2,1,0:T(1,128)} %copy.183), calls=%async_computation.1 | async-start | bytes 65536 | tf_op jit(solution)/shard_map/all_to_all | solution.py:48
  29.7 8.5 %all-to-all-done.1 = s32[64,1,1]{2,1,0:T(1,128)S(1)} async-done(((s32[64,1,1]{2,1,0:T(1,128)}), s32[64,1,1]{2,1,0:T(1,128)S(1)}, u32[]{:S(2)}, u32[]{:S(2)}) %all-to-all-start.1) | async-done | bytes 288 | tf_op jit(solution)/shard_map/all_to_all | solution.py:48
  38.1 4.6 %all-to-all-start = ((bf16[64,4,256]{2,1,0:T(4,128)(2,1)}), bf16[64,4,256]{2,1,0:T(4,128)(2,1)S(1)}, u32[]{:S(2)}, u32[]{:S(2)}) async-start(bf16[64,4,256]{2,1,0:T(4,128)(2,1)} %reshape.379), calls=%async_computation | async-start | bytes 262144 | tf_op jit(solution)/shard_map/all_to_all | solution.py:41
  46.7 1.9 collective-permute-start.5
  48.6 2.4 collective-permute-start.4
  53.6 3.4 collective-permute-start.6
  58.3 4.2 collective-permute-done.7
  69.9 1.9 collective-permute-start
  73.9 13.0 %all-to-all-start.2 = ((bf16[64,4,256]{2,1,0:T(4,128)(2,1)}), bf16[64,4,256]{2,1,0:T(4,128)(2,1)S(1)}, u32[]{:S(2)}, u32[]{:S(2)}) async-start(bf16[64,4,256]{2,1,0:T(4,128)(2,1)} %reshape.436), calls=%async_computation.2 | async-start | bytes 262144 | tf_op jit(solution)/shard_map/all_to_all | solution.py:107
  87.1 3.4 collective-permute-start.1
  91.9 3.2 collective-permute-start.2
  97.5 2.4 all-to-all-done.2
  107.8 1.6 copy.166
  110.4 1.6 copy.156
  113.6 1.6 copy.167
  116.8 1.6 copy.165
  120.0 1.6 copy.164
  123.2 1.6 copy.162
  139.3 1.7 fusion.105
  141.0 1.8 fusion.29
  169.8 74.8 %all-reduce.5.cloned.1.call-done = f32[6912,128]{1,0:T(8,128)} async-done(((f32[6912,128]{1,0:T(8,128)}), f32[6912,128]{1,0:T(8,128)}) %all-reduce.5.cloned.1.call-update) | async-done | bytes 3538960 | tf_op jit(solution)/shard_map/psum | solution.py:104
  245.8 1.6 copy.181
  272.9 146.2 %all-reduce.7.cloned.1.call-done = f32[6912,128]{1,0:T(8,128)} async-done(((f32[6912,128]{1,0:T(8,128)}), f32[6912,128]{1,0:T(8,128)}) %all-reduce.7.cloned.1.call-update) | async-done | bytes 3538960 | tf_op jit(solution)/shard_map/psum | solution.py:104
  419.2 3.4 multiply_convert_fusion
  (245 shorter events, 109.4 us)
Async XLA Ops:
  9.6 28.5 %all-to-all-start.1 = ((s32[64,1,1]{2,1,0:T(1,128)}), s32[64,1,1]{2,1,0:T(1,128)S(1)}, u32[]{:S(2)}, u32[]{:S(2)}) async-start(s32[64,1,1]{2,1,0:T(1,128)} %copy.183), calls=%async_computation.1 | async-start | bytes 65536 | tf_op jit(solution)/shard_map/all_to_all | solution.py:48
  38.1 30.2 %all-to-all-start = ((bf16[64,4,256]{2,1,0:T(4,128)(2,1)}), bf16[64,4,256]{2,1,0:T(4,128)(2,1)S(1)}, u32[]{:S(2)}, u32[]{:S(2)}) async-start(bf16[64,4,256]{2,1,0:T(4,128)(2,1)} %reshape.379), calls=%async_computation | async-start | bytes 262144 | tf_op jit(solution)/shard_map/all_to_all | solution.py:41
  42.7 20.3 %copy-start = (bf16[27,256,128]{2,1,0:T(8,128)(2,1)S(1)}, bf16[27,256,128]{2,1,0:T(8,128)(2,1)}, u32[]{:S(2)}) copy-start(bf16[27,256,128]{2,1,0:T(8,128)(2,1)} %param.8) | copy-start | bytes 5308420
  46.7 5.3 %collective-permute-start.5 = (bf16[1,8,4,128]{3,2,1,0:T(4,128)(2,1)S(1)}, bf16[1,8,4,128]{3,2,1,0:T(4,128)(2,1)S(1)}, u32[]{:S(2)}, u32[]{:S(2)}) collective-permute-start(bf16[1,8,4,128]{3,2,1,0:T(4,128)(2,1)S(1)} %bitcast.495), channel_id=1, source_target_pairs={{64,0},{128,64},{192,128},{256,192},{320,256},{384,320},{448,384},... | collective-permute-start | bytes 24584 | tf_op jit(solution)/shard_map/ppermute | solution.py:18
  48.6 5.0 %collective-permute-start.4 = (bf16[1,8,4,128]{3,2,1,0:T(4,128)(2,1)S(1)}, bf16[1,8,4,128]{3,2,1,0:T(4,128)(2,1)S(1)}, u32[]{:S(2)}, u32[]{:S(2)}) collective-permute-start(bf16[1,8,4,128]{3,2,1,0:T(4,128)(2,1)S(1)} %bitcast.494), channel_id=1, source_target_pairs={{0,64},{64,128},{128,192},{192,256},{256,320},{320,384},{384,448},... | collective-permute-start | bytes 24584 | tf_op jit(solution)/shard_map/ppermute | solution.py:16
  53.6 4.7 %collective-permute-start.6 = (bf16[10,1,4,128]{3,2,1,0:T(4,128)(2,1)S(1)}, bf16[10,1,4,128]{3,2,1,0:T(4,128)(2,1)S(1)}, u32[]{:S(2)}, u32[]{:S(2)}) collective-permute-start(bf16[10,1,4,128]{3,2,1,0:T(4,128)(2,1)S(1)} %get-tuple-element.65), channel_id=1, source_target_pairs={{0,1},{1,2},{2,3},{3,4},{4,5},{5,6},{6,7},{7,8},{8,9},{9,10},{10,1... | collective-permute-start | bytes 30728 | tf_op jit(solution)/shard_map/ppermute | solution.py:16
  56.9 5.6 %collective-permute-start.7 = (bf16[10,1,4,128]{3,2,1,0:T(4,128)(2,1)S(1)}, bf16[10,1,4,128]{3,2,1,0:T(4,128)(2,1)S(1)}, u32[]{:S(2)}, u32[]{:S(2)}) collective-permute-start(bf16[10,1,4,128]{3,2,1,0:T(4,128)(2,1)S(1)} %get-tuple-element.66), channel_id=1, source_target_pairs={{1,0},{2,1},{3,2},{4,3},{5,4},{6,5},{7,6},{8,7},{9,8},{10,9},{11,1... | collective-permute-start | bytes 30728 | tf_op jit(solution)/shard_map/ppermute | solution.py:18
  69.9 20.5 %collective-permute-start = (bf16[1,8,4,256]{3,1,2,0:T(8,128)(2,1)S(1)}, bf16[1,8,4,256]{3,1,2,0:T(8,128)(2,1)S(1)}, u32[]{:S(2)}, u32[]{:S(2)}) collective-permute-start(bf16[1,8,4,256]{3,1,2,0:T(8,128)(2,1)S(1)} %copy.152), channel_id=1, source_target_pairs={{0,64},{64,128},{128,192},{192,256},{256,320},{320,384},{384,448},... | collective-permute-start | bytes 49160 | tf_op jit(solution)/shard_map/ppermute | solution.py:16
  73.9 26.1 %all-to-all-start.2 = ((bf16[64,4,256]{2,1,0:T(4,128)(2,1)}), bf16[64,4,256]{2,1,0:T(4,128)(2,1)S(1)}, u32[]{:S(2)}, u32[]{:S(2)}) async-start(bf16[64,4,256]{2,1,0:T(4,128)(2,1)} %reshape.436), calls=%async_computation.2 | async-start | bytes 262144 | tf_op jit(solution)/shard_map/all_to_all | solution.py:107
  86.9 157.7 %all-reduce.5.cloned.1.call-start = ((), (), s32[]{:S(2)}) async-start(), calls=%async_computation.3 | async-start | bytes 7077888 | tf_op jit(solution)/shard_map/psum | solution.py:104
  87.0 9.6 %copy-start.15 = (bf16[8,8,4,256]{3,2,1,0:T(4,128)(2,1)}, bf16[8,8,4,256]{3,2,1,0:T(4,128)(2,1)S(1)}, u32[]{:S(2)}) copy-start(bf16[8,8,4,256]{3,2,1,0:T(4,128)(2,1)S(1)} %reshape.381) | copy-start | bytes 393220
  87.1 4.8 %collective-permute-start.1 = (bf16[1,8,4,256]{3,1,2,0:T(8,128)(2,1)S(1)}, bf16[1,8,4,256]{3,1,2,0:T(8,128)(2,1)S(1)}, u32[]{:S(2)}, u32[]{:S(2)}) collective-permute-start(bf16[1,8,4,256]{3,1,2,0:T(8,128)(2,1)S(1)} %copy.153), channel_id=1, source_target_pairs={{64,0},{128,64},{192,128},{256,192},{320,256},{384,320},{448,384},... | collective-permute-start | bytes 49160 | tf_op jit(solution)/shard_map/ppermute | solution.py:18
  90.5 11.0 %copy-start.29 = (bf16[9,8,4,256]{3,1,2,0:T(8,128)(2,1)}, bf16[9,8,4,256]{3,1,2,0:T(8,128)(2,1)S(1)}, u32[]{:S(2)}) copy-start(bf16[9,8,4,256]{3,1,2,0:T(8,128)(2,1)S(1)} %get-tuple-element.53) | copy-start | bytes 442372
  91.8 9.6 %copy-start.23 = (bf16[9,8,4,256]{3,1,2,0:T(8,128)(2,1)}, bf16[9,8,4,256]{3,1,2,0:T(8,128)(2,1)S(1)}, u32[]{:S(2)}) copy-start(bf16[9,8,4,256]{3,1,2,0:T(8,128)(2,1)S(1)} %get-tuple-element.71) | copy-start | bytes 442372
  91.9 9.6 %collective-permute-start.2 = (bf16[10,1,4,256]{3,1,2,0:T(2,128)(2,1)S(1)}, bf16[10,1,4,256]{3,1,2,0:T(2,128)(2,1)S(1)}, u32[]{:S(2)}, u32[]{:S(2)}) collective-permute-start(bf16[10,1,4,256]{3,1,2,0:T(2,128)(2,1)S(1)} %get-tuple-element.50), channel_id=1, source_target_pairs={{0,1},{1,2},{2,3},{3,4},{4,5},{5,6},{6,7},{7,8},{8,9},{9,10},{10,1... | collective-permute-start | bytes 61448 | tf_op jit(solution)/shard_map/ppermute | solution.py:16
  95.1 6.4 %collective-permute-start.3 = (bf16[10,1,4,256]{3,1,2,0:T(2,128)(2,1)S(1)}, bf16[10,1,4,256]{3,1,2,0:T(2,128)(2,1)S(1)}, u32[]{:S(2)}, u32[]{:S(2)}) collective-permute-start(bf16[10,1,4,256]{3,1,2,0:T(2,128)(2,1)S(1)} %get-tuple-element.51), channel_id=1, source_target_pairs={{1,0},{2,1},{3,2},{4,3},{5,4},{6,5},{7,6},{8,7},{9,8},{10,9},{11,1... | collective-permute-start | bytes 61448 | tf_op jit(solution)/shard_map/ppermute | solution.py:18
  164.9 4.3 %copy-start.7 = (bf16[256,256]{1,0:T(8,128)(2,1)S(1)}, bf16[256,256]{1,0:T(8,128)(2,1)}, u32[]{:S(2)}) copy-start(bf16[256,256]{1,0:T(8,128)(2,1)} %reshape.390) | copy-start | bytes 393220
  165.0 4.5 %copy-start.6 = (bf16[256,256]{1,0:T(8,128)(2,1)S(1)}, bf16[256,256]{1,0:T(8,128)(2,1)}, u32[]{:S(2)}) copy-start(bf16[256,256]{1,0:T(8,128)(2,1)} %reshape.391) | copy-start | bytes 393220
  165.0 254.2 %all-reduce.7.cloned.1.call-start = ((), (), s32[]{:S(2)}) async-start(), calls=%async_computation.4 | async-start | bytes 7077888 | tf_op jit(solution)/shard_map/psum | solution.py:104
  244.7 13.4 %copy-start.3 = (bf16[8,8,4,256]{3,1,2,0:T(8,128)(2,1)S(1)}, bf16[8,8,4,256]{3,1,2,0:T(8,128)(2,1)}, u32[]{:S(2)}) copy-start(bf16[8,8,4,256]{3,1,2,0:T(8,128)(2,1)} %get-tuple-element.6) | copy-start | bytes 393220
  244.7 15.0 %copy-start.2 = (bf16[8,8,4,256]{3,1,2,0:T(8,128)(2,1)S(1)}, bf16[8,8,4,256]{3,1,2,0:T(8,128)(2,1)}, u32[]{:S(2)}) copy-start(bf16[8,8,4,256]{3,1,2,0:T(8,128)(2,1)} %get-tuple-element.7) | copy-start | bytes 393220
  244.7 16.7 %copy-start.1 = (bf16[8,8,4,256]{3,1,2,0:T(8,128)(2,1)S(1)}, bf16[8,8,4,256]{3,1,2,0:T(8,128)(2,1)}, u32[]{:S(2)}) copy-start(bf16[8,8,4,256]{3,1,2,0:T(8,128)(2,1)} %get-tuple-element.8) | copy-start | bytes 393220
  264.6 5.7 %copy-start.12 = (bf16[256,256]{1,0:T(8,128)(2,1)S(1)}, bf16[256,256]{1,0:T(8,128)(2,1)}, u32[]{:S(2)}) copy-start(bf16[256,256]{1,0:T(8,128)(2,1)} %reshape.397) | copy-start | bytes 393220
  264.6 5.8 %copy-start.14 = (bf16[256,256]{1,0:T(8,128)(2,1)S(1)}, bf16[256,256]{1,0:T(8,128)(2,1)}, u32[]{:S(2)}) copy-start(bf16[256,256]{1,0:T(8,128)(2,1)} %reshape.398) | copy-start | bytes 393220
  (20 other events, 41.9 us)
Sparse Core Ops, SparseCore 0:
  165.1 79.5 all-reduce.4
  248.4 170.7 all-reduce.6
